TPU v7x, 128 devices: a whole 4x4x4 slice. The times are simulated.
128 devices in a mesh: req: 16 (over z, y), mlp: 8 (over x, core).
Axes of the slice: x: 4, y: 4, z: 4, core: 2. Of those that a mesh axis runs over, the one named last changes fastest.
Arguments:
- activations: bfloat16 [8192, 4096], P('req', 'mlp')
- slot_segment: int32 [8192], P('req'), may hold values from -1 to 511, as said below
- attn_norm_gain: float32 [4096], replicated, may hold values from 0.5 to 1.5
- attn_norm_bias: float32 [4096], replicated, may hold values from -1.5 to 1.5
- mlp_norm_gain: float32 [4096], replicated, may hold values from 0.5 to 1.5
- mlp_norm_bias: float32 [4096], replicated, may hold values from -1.5 to 1.5
- qkv_weight: bfloat16 [4096, 6144], P(None, 'mlp')
- dense_weight: bfloat16 [2048, 4096], P('mlp'), may hold values from -0.1875 to 0.1875
- fc_weight: bfloat16 [4096, 8192], P(None, 'mlp'), may hold values from -0.09375 to 0.09375
- proj_weight: bfloat16 [8192, 4096], P('mlp'), may hold values from -0.09375 to 0.09375
Outputs:
- output_rows: float32 [8192, 4096], P('req', 'mlp')
- cache_rows: bfloat16 [2, 4096, 2048], P(None, 'req', 'mlp')
Inputs may be any that keep to these rules, and one draw needn't show every extreme that they name: `slot_segment`: each group's 512 slots hold live slots first and -1 after them; the live count of every group is a multiple of 16 between 16 and 512, the counts of all groups sum to 4096, and some group is full, its last slot beginning a prompt of one token. A live slot holds the group slot where its prompt begins; a prompt's slots are consecutive.
All inputs are finite; a program needn't handle non-finite values.
Results may differ from a plain program's by a relative error of at most 0.0047.
The roundings to bfloat16 on the way count: a program that leaves them out, or rounds other values in their place, can miss the bound.
Values may be sent and summed in bfloat16 or wider, within the bound.
A program may use at most 128 MiB of HBM per device.

v0:
```python
import jax
import jax.numpy as jnp
from jax import lax
from jax.sharding import PartitionSpec as P

HD = 128
ROT = 32
LIVE_DEV = 256


def layer_norm(row_data, gain_vec, bias_vec):
    row_data = row_data.astype(jnp.float32)
    row_mean = jnp.mean(row_data, axis=-1, keepdims=True)
    centered = row_data - row_mean
    variance = jnp.mean(centered * centered, axis=-1, keepdims=True)
    return (centered * lax.rsqrt(variance + 1e-05) * gain_vec + bias_vec).astype(jnp.bfloat16)


def rotate(head_data, position):
    half_rot = ROT // 2
    inv_freq = 10000.0 ** (-(jnp.arange(half_rot).astype(jnp.float32) * 2.0 / ROT))
    angles = position.astype(jnp.float32)[:, None] * inv_freq[None, :]
    cosine = jnp.concatenate([jnp.cos(angles), jnp.cos(angles)], axis=-1)[:, None, :]
    sine_part = jnp.concatenate([jnp.sin(angles), jnp.sin(angles)], axis=-1)[:, None, :]
    rot_part = head_data[..., :ROT]
    pass_part = head_data[..., ROT:]
    first_half = rot_part[..., :half_rot]
    second = rot_part[..., half_rot:]
    turned = jnp.concatenate([-second, first_half], axis=-1)
    return jnp.concatenate([rot_part * cosine + turned * sine_part, pass_part], axis=-1)


def attend(normed, segment, qkv_weight):
    slot_count = normed.shape[0]
    head_count = qkv_weight.shape[1] // (3 * HD)
    mixed_proj = jnp.dot(normed, qkv_weight, preferred_element_type=jnp.float32).reshape(
        slot_count, head_count, 3, HD
    )
    slot_index = jnp.arange(slot_count, dtype=jnp.int32)
    position = slot_index - segment
    query_rows = rotate(mixed_proj[:, :, 0], position).astype(jnp.bfloat16)
    key_rows = rotate(mixed_proj[:, :, 1], position).astype(jnp.bfloat16)
    value_rows = mixed_proj[:, :, 2].astype(jnp.bfloat16)
    scores = jnp.einsum(
        "qhd,khd->hqk", query_rows, key_rows, preferred_element_type=jnp.float32
    ) * HD ** (-0.5)
    allowed = (
        (segment[:, None] == segment[None, :])
        & (slot_index[None, :] <= slot_index[:, None])
        & (segment[:, None] >= 0)
    )
    scores = jnp.where(allowed[None], scores, -1e30)
    row_max = jnp.max(scores, axis=-1, keepdims=True)
    weights = jnp.exp(scores - row_max)
    prob_rows = (weights / jnp.sum(weights, axis=-1, keepdims=True)).astype(jnp.bfloat16)
    context = jnp.einsum("hqk,khd->qhd", prob_rows, value_rows, preferred_element_type=jnp.float32)
    context = context.astype(jnp.bfloat16).reshape(slot_count, head_count * HD)
    return (
        context,
        key_rows.reshape(slot_count, head_count * HD),
        value_rows.reshape(slot_count, head_count * HD),
    )


def body(
    activations,
    slot_segment,
    attn_norm_gain,
    attn_norm_bias,
    mlp_norm_gain,
    mlp_norm_bias,
    qkv_weight,
    dense_weight,
    fc_weight,
    proj_weight,
):
    slot_count = activations.shape[0]
    groups = lax.axis_size("req")
    per_peer = slot_count // groups
    live_slot = slot_segment >= 0
    group_fill = lax.all_gather(
        jnp.sum(live_slot.astype(jnp.int32)).reshape(1), "req", axis=0, tiled=True
    )
    group_units = group_fill // groups
    received_live = (jnp.arange(per_peer, dtype=jnp.int32)[None, :] < group_units[:, None]).reshape(
        -1
    )
    live_rank = jnp.cumsum(received_live.astype(jnp.int32)) - 1
    target = jnp.where(received_live, live_rank, LIVE_DEV)
    pick_rows = (
        jnp.zeros((LIVE_DEV,), jnp.int32)
        .at[target]
        .set(jnp.arange(groups * per_peer, dtype=jnp.int32), mode="drop")
    )
    full_rows = lax.all_gather(activations, "mlp", axis=1, tiled=True)
    normed = layer_norm(full_rows, attn_norm_gain, attn_norm_bias)
    context, key_rows, value_rows = attend(normed, slot_segment, qkv_weight)
    key_value = jnp.concatenate([key_rows, value_rows], axis=1).reshape(per_peer, groups, -1)
    cache_rows = lax.all_to_all(key_value, "req", split_axis=1, concat_axis=0, tiled=True)
    cache_rows = jnp.take(cache_rows.reshape(groups * per_peer, -1), pick_rows, axis=0)
    width = key_rows.shape[1]
    cache_rows = jnp.stack([cache_rows[:, :width], cache_rows[:, width:]])
    mlp_normed = layer_norm(full_rows, mlp_norm_gain, mlp_norm_bias)
    hidden = jax.nn.gelu(
        jnp.dot(mlp_normed, fc_weight, preferred_element_type=jnp.float32), approximate=False
    )
    hidden = hidden.astype(jnp.bfloat16)
    part = jnp.dot(context, dense_weight, preferred_element_type=jnp.float32) + jnp.dot(
        hidden, proj_weight, preferred_element_type=jnp.float32
    )
    total = lax.psum_scatter(
        part.astype(jnp.bfloat16), "mlp", scatter_dimension=1, tiled=True
    ).astype(jnp.float32)
    combined = activations.astype(jnp.float32) + total
    output_rows = jnp.where(live_slot[:, None], combined, 0.0)
    return (output_rows, cache_rows)


def solution(mesh):
    placed = (
        P("req", "mlp"),
        P("req"),
        P(),
        P(),
        P(),
        P(),
        P(None, "mlp"),
        P("mlp", None),
        P(None, "mlp"),
        P("mlp", None),
    )
    return jax.shard_map(
        body,
        mesh=mesh,
        in_specs=placed,
        out_specs=(P("req", "mlp"), P(None, "req", "mlp")),
        check_vma=False,
    )
```

profile of v0, /device:TPU:0, one launch (start us, length us, event | category | flops | bytes accessed | tf_op | source)
XLA Modules:
  0.0 147.7 jit_solution(17991416886373539449)
XLA Ops:
  7.2 0.7 all-gather.2.cloned.1.call-update
  8.0 1.3 convert_reduce_fusion.1
  9.7 0.8 copy.49
  10.5 1.0 fusion.71
  11.5 1.0 copy.46
  12.6 31.7 %all-gather.2.cloned.1.call-done = bf16[512,4096]{1,0:T(8,128)(2,1)} async-done(((bf16[512,512]{1,0:T(8,128)(2,1)}), bf16[512,4096]{1,0:T(8,128)(2,1)}) %all-gather.2.cloned.1.call-update) | async-done | bytes 4194320 | tf_op jit(solution)/shard_map/all_gather | solution.py:95
  44.3 3.0 %convert_reduce_fusion = f32[512]{0:T(512)S(1)} fusion(bf16[512,4096]{1,0:T(8,128)(2,1)} %all-gather.2.cloned.1.call-done), kind=kLoop, calls=%fused_computation.4 | loop fusion | flops 4193792 | bytes 4196352 | tf_op jit(solution)/shard_map/reduce_sum | solution.py:13
  47.3 0.5 copy-done.1
  47.7 1.2 fusion.9
  49.0 6.6 %fusion.12 = f32[512,768]{0,1:T(8,128)S(1)} fusion(bf16[4096,768]{1,0:T(8,128)(2,1)} %param.16, bf16[512,4096]{1,0:T(8,128)(2,1)S(1)} %copy-done.1, f32[4096]{0:T(1024)S(1)} %copy-done.10, f32[4096]{0:T(1024)S(1)} %copy-done.11, f32[512]{0:T(512)S(1)} %add_rsqrt_fusion, f32[512]{0:T(512)S(1)} %broadcast_multiply_fusion), kind=kOutput, calls=%fused_computation.16 | convolution fusion | flops 3233808384 | bytes 12095488 | tf_op jit(solution)/shard_map/dot_general | solution.py:36
  55.6 0.8 fusion.76
  56.3 0.9 fusion.137
  57.4 0.9 slice.78
  58.2 1.1 slice_negate_fusion
  59.4 1.2 copy.58
  60.7 0.8 slice.98
  62.9 0.7 copy-done.8
  63.6 2.1 %fusion.138 = f32[2,512]{1,0:T(2,128)S(1)} fusion(pred[512,512]{0,1:T(8,128)(4,1)} %copy.46, bf16[512,2,128]{2,0,1:T(8,128)(2,1)S(1)} %maximum_convert_fusion, bf16[512,2,96]{2,0,1:T(8,128)(2,1)} %slice.98, bf16[512,2,32]{2,0,1:T(8,128)(2,1)S(1)} %fusion.75), kind=kOutput, calls=%fused_computation.173 | convolution fusion | flops 136839680 | bytes 790528 | tf_op jit(solution)/shard_map/sub | solution.py:54
  65.8 2.3 %convolution_convert_fusion = bf16[2,128,512]{2,1,0:T(8,128)(2,1)S(1)} fusion(f32[2,512]{1,0:T(2,128)S(1)} %fusion.138, bf16[512,2,1,128]{0,3,1,2:T(8,128)(2,1)S(1)} %copy-done.7, pred[512,512]{0,1:T(8,128)(4,1)} %copy.46, bf16[512,2,128]{2,0,1:T(8,128)(2,1)S(1)} %maximum_convert_fusion, bf16[512,2,96]{2,0,1:T(8,128)(2,1)S(1)} %copy-done.9, ...), kind=kOutput, calls=%fused_computation.49 | convolution fusion | flops 271713792 | bytes 1314816 | tf_op jit(solution)/shard_map/hqk,khd->qhd/dot_general | solution.py:56
  68.1 23.6 %fusion.35 = f32[512,4096]{1,0:T(8,128)} fusion(bf16[1024,4096]{1,0:T(8,128)(2,1)} %param.19, bf16[4096,1024]{1,0:T(8,128)(2,1)} %param.18, bf16[512,4096]{1,0:T(8,128)(2,1)} %all-gather.2.cloned.1.call-done, f32[4096]{0:T(1024)S(1)} %copy-done.12, f32[4096]{0:T(1024)S(1)} %copy-done.13, f32[512]{0:T(512)S(1)} %add_rsqrt_fusion, ...), kind=kOutput, calls=%fused_computation.47 | convolution fusion | flops 8636596224 | bytes 29396992 | tf_op jit(solution)/shard_map/dot_general | solution.py:108
  91.7 6.6 %add_convert_fusion = bf16[512,4096]{1,0:T(8,128)(2,1)} fusion(f32[512,4096]{1,0:T(8,128)} %fusion.35, bf16[512,256]{0,1:T(8,128)(2,1)S(1)} %bitcast.45, bf16[256,4096]{1,0:T(8,128)(2,1)S(1)} %copy-done), kind=kOutput, calls=%fused_computation.14 | convolution fusion | flops 1077936128 | bytes 14942208 | tf_op jit(solution)/shard_map/dot_general | solution.py:108
  98.4 0.6 copy-done.14
  99.0 0.6 dynamic-slice
  99.6 1.4 dynamic-update-slice
  101.0 16.5 %all-reduce = s32[16]{0:T(128)S(1)} all-reduce(s32[16]{0:T(128)S(1)} %dynamic-update-slice), channel_id=1, replica_groups=mesh['req'=16,'mlp'=8] {'req'}, use_global_device_ids=true, to_apply=%add | all-reduce | flops 16 | bytes 128
  118.6 2.4 %scatter_custom_fusion = s32[256]{0:T(256)S(1)} fusion(s32[512]{0:T(512)S(1)} %bitcast.47, s32[512]{0:T(512)S(1)} %iota.32, s32[]{:T(128)} %constant.46.clone.1), kind=kCustom, calls=%fused_computation.131 | custom fusion | bytes 1028 | tf_op jit(solution)/shard_map/scatter | solution.py:93
  121.9 1.1 copy.54
  123.0 3.6 %all-to-all-start = ((bf16[32,16,512]{2,0,1:T(8,128)(2,1)}), bf16[32,16,512]{2,0,1:T(8,128)(2,1)S(1)}, u32[]{:S(2)}, u32[]{:S(2)}) async-start(bf16[32,16,512]{2,0,1:T(8,128)(2,1)} %copy.54), calls=%async_computation.1 | async-start | bytes 1048576 | tf_op jit(solution)/shard_map/all_to_all | solution.py:99
  126.6 10.1 %all-to-all-done = bf16[32,16,512]{2,0,1:T(8,128)(2,1)S(1)} async-done(((bf16[32,16,512]{2,0,1:T(8,128)(2,1)}), bf16[32,16,512]{2,0,1:T(8,128)(2,1)S(1)}, u32[]{:S(2)}, u32[]{:S(2)}) %all-to-all-start) | async-done | bytes 524320 | tf_op jit(solution)/shard_map/all_to_all | solution.py:99
  136.7 1.2 gather_fusion
  138.0 0.7 pad_maximum_fusion.1
  138.7 2.2 %add_select_fusion = f32[512,512]{1,0:T(8,128)} fusion(bf16[512,512]{1,0:T(8,128)(2,1)} %reduce-scatter.2.cloned.1.call-done, bf16[512,512]{1,0:T(8,128)(2,1)S(1)} %copy-done.3, pred[512]{0:T(512)(128)(4,1)S(1)} %get-tuple-element.3), kind=kLoop, calls=%fused_computation.50 | loop fusion | flops 1048576 | bytes 2097664 | tf_op jit(solution)/shard_map/jit(_where)/select_n | solution.py:115
  (69 shorter events, 4.2 us)
Async XLA Ops:
  7.2 84.6 %copy-start = (bf16[256,4096]{1,0:T(8,128)(2,1)S(1)}, bf16[256,4096]{1,0:T(8,128)(2,1)}, u32[]{:S(2)}) copy-start(bf16[256,4096]{1,0:T(8,128)(2,1)} %param.17) | copy-start | bytes 6291460
  7.2 37.1 %all-gather.2.cloned.1.call-start = ((), (), s32[]{:S(2)}) async-start(), calls=%async_computation.2 | async-start | bytes 4718592 | tf_op jit(solution)/shard_map/all_gather | solution.py:95
  7.9 130.8 %reduce-scatter.2.cloned.1.call-start = ((), (), s32[]{:S(2)}) async-start(), calls=%async_computation.3 | async-start | bytes 4718592 | tf_op jit(solution)/shard_map/reduce_scatter | solution.py:111
  44.3 3.4 %copy-start.1 = (bf16[512,4096]{1,0:T(8,128)(2,1)S(1)}, bf16[512,4096]{1,0:T(8,128)(2,1)}, u32[]{:S(2)}) copy-start(bf16[512,4096]{1,0:T(8,128)(2,1)} %all-gather.2.cloned.1.call-done) | copy-start | bytes 12582916
  47.7 1.2 copy-start.10
  47.7 1.2 copy-start.11
  60.6 1.1 copy-start.2
  60.6 1.2 copy-start.4
  60.7 1.4 copy-start.5
  61.5 1.0 copy-start.6
  62.9 0.7 copy-start.8
  63.6 2.1 %copy-start.7 = (bf16[512,2,1,128]{0,3,1,2:T(8,128)(2,1)S(1)}, bf16[512,2,1,128]{0,3,1,2:T(8,128)(2,1)}, u32[]{:S(2)}) copy-start(bf16[512,2,1,128]{0,3,1,2:T(8,128)(2,1)} %fusion.76) | copy-start | bytes 786436
  63.6 2.1 %copy-start.9 = (bf16[512,2,96]{2,0,1:T(8,128)(2,1)S(1)}, bf16[512,2,96]{2,0,1:T(8,128)(2,1)}, u32[]{:S(2)}) copy-start(bf16[512,2,96]{2,0,1:T(8,128)(2,1)} %slice.98) | copy-start | bytes 589828
  65.7 2.3 %copy-start.12 = (f32[4096]{0:T(1024)S(1)}, f32[4096]{0:T(1024)}, u32[]{:S(2)}) copy-start(f32[4096]{0:T(1024)} %param.15) | copy-start | bytes 49156
  65.8 2.3 %copy-start.13 = (f32[4096]{0:T(1024)S(1)}, f32[4096]{0:T(1024)}, u32[]{:S(2)}) copy-start(f32[4096]{0:T(1024)} %param.14) | copy-start | bytes 49156
  98.4 0.7 copy-start.14
  123.0 13.7 %all-to-all-start = ((bf16[32,16,512]{2,0,1:T(8,128)(2,1)}), bf16[32,16,512]{2,0,1:T(8,128)(2,1)S(1)}, u32[]{:S(2)}, u32[]{:S(2)}) async-start(bf16[32,16,512]{2,0,1:T(8,128)(2,1)} %copy.54), calls=%async_computation.1 | async-start | bytes 1048576 | tf_op jit(solution)/shard_map/all_to_all | solution.py:99
  126.6 12.1 %copy-start.3 = (bf16[512,512]{1,0:T(8,128)(2,1)S(1)}, bf16[512,512]{1,0:T(8,128)(2,1)}, u32[]{:S(2)}) copy-start(bf16[512,512]{1,0:T(8,128)(2,1)} %param.10) | copy-start | bytes 1572868
Sparse Core Ops, SparseCore 0:
  9.7 34.5 all-gather.1
  98.5 38.3 reduce-scatter.1
where the time goes:
time: 148 us
  waiting for transfers between devices  42.5 us (29%)
  matrix products  41.2 us (28%)
  local copies, waits for them, and re-layouts  17.2 us (12%)
  blocking collectives  16.5 us (11%)
  between operations  14.4 us (10%)
  other arithmetic  12.3 us (8%)
  starting transfers between devices  3.65 us (2%)
    all_gather x1, waiting for transfers between devices, body(): full_rows = lax.all_gather(activations, 'mlp', axis=1, tiled=True)  31.7 us
    dot_general x1, matrix products, body(): jnp.dot(hidden, proj_weight, preferred_element_type=jnp.float32)  23.6 us
    unnamed x1, blocking collectives  16.5 us
    all_to_all x1, waiting for transfers between devices, body(): lax.all_to_all(key_value, 'req', split_axis=1, concat_axis=0, tiled=True)  10.1 us
    dot_general x1, matrix products, body(): jnp.dot(context, dense_weight, preferred_element_type=jnp.float32)  6.64 us
    dot_general x1, matrix products, attend(): jnp.dot(normed, qkv_weight, preferred_element_type=jnp.float32)  6.56 us
    unnamed x35, local copies, waits for them, and re-layouts  5.81 us
    all_to_all x1, starting transfers between devices, body(): lax.all_to_all(key_value, 'req', split_axis=1, concat_axis=0, tiled=True)  3.57 us
  transfers between devices with their start and end apart: 3, of which 2 were waited for; matrix products, arithmetic and copies ran while one was open for 9% of the time, Pallas kernels for 0%

commit v1 on v0

--- a/solution.py
+++ b/solution.py
@@ -92,7 +92,10 @@
         .at[target]
         .set(jnp.arange(groups * per_peer, dtype=jnp.int32), mode="drop")
     )
-    full_rows = lax.all_gather(activations, "mlp", axis=1, tiled=True)
+    full_rows = jnp.concatenate(
+        lax.all_to_all(jnp.stack([activations for _ in range(lax.axis_size("mlp"))]), "mlp", 0, 0),
+        axis=1,
+    )
     normed = layer_norm(full_rows, attn_norm_gain, attn_norm_bias)
     context, key_rows, value_rows = attend(normed, slot_segment, qkv_weight)
     key_value = jnp.concatenate([key_rows, value_rows], axis=1).reshape(per_peer, groups, -1)

time: 148 us -> 174 us (1.18)
  local copies, waits for them, and re-layouts: 17.2 us -> 31.5 us
  waiting for transfers between devices: 42.5 us -> 49.3 us
  starting transfers between devices: 3.65 us -> 8.33 us
  matrix products: 41.2 us -> 38 us
    all_to_all x0 -> x1, waiting for transfers between devices: none -> 39.3 us  [body(): lax.all_to_all(jnp.stack([activations for _ in range(lax.axis_size('mlp')...]
    all_gather x1 -> x0, waiting for transfers between devices: 31.7 us -> none  [body(): full_rows = lax.all_gather(activations, 'mlp', axis=1, tiled=True)]
    unnamed x35 -> x30, local copies, waits for them, and re-layouts: 5.81 us -> 13.8 us
    all_to_all x0 -> x1, local copies, waits for them, and re-layouts: none -> 6.52 us  [body(): lax.all_to_all(jnp.stack([activations for _ in range(lax.axis_size('mlp')...]
    all_to_all x0 -> x1, starting transfers between devices: none -> 4.71 us  [body(): lax.all_to_all(jnp.stack([activations for _ in range(lax.axis_size('mlp')...]
    convert_element_type x0 -> x2, other arithmetic: none -> 4.64 us  [layer_norm(): (centered * lax.rsqrt(variance + 1e-05) * gain_vec + bias_vec).astype(jnp...]
    another operation x1 -> x2, local copies, waits for them, and re-layouts: 0.12 us -> 3.7 us  [the longest x1 3.59 us: body(): jnp.stack([activations for _ in range(lax.axis_size('mlp'))])]
    dot_general x1, matrix products: 6.56 us -> 3.4 us  [attend(): jnp.dot(normed, qkv_weight, preferred_element_type=jnp.float32)]
  transfers between devices with their start and end apart: 3 -> 3, of which waited for: 2 -> 2; matrix products, arithmetic and copies ran while one was open for 9% -> 12% of each run, Pallas kernels for 0% -> 0%
where the time goes in v1:
time: 174 us; the launch traced here: 173 us
  waiting for transfers between devices  49.3 us (28%)
  matrix products  38 us (22%)
  local copies, waits for them, and re-layouts  31.5 us (18%)
  blocking collectives  17.8 us (10%)
  between operations  14.3 us (8%)
  other arithmetic  13.6 us (8%)
  starting transfers between devices  8.33 us (5%)
    all_to_all x1, waiting for transfers between devices, body(): lax.all_to_all(jnp.stack([activations for _ in range(lax.axis_size('mlp')...  39.3 us
    dot_general x1, matrix products, body(): jnp.dot(hidden, proj_weight, preferred_element_type=jnp.float32)  23.4 us
    unnamed x1, blocking collectives  17.8 us
    unnamed x30, local copies, waits for them, and re-layouts  13.8 us
    all_to_all x1, waiting for transfers between devices, body(): lax.all_to_all(key_value, 'req', split_axis=1, concat_axis=0, tiled=True)  10.1 us
    dot_general x1, matrix products, body(): jnp.dot(context, dense_weight, preferred_element_type=jnp.float32)  6.64 us
    all_to_all x1, local copies, waits for them, and re-layouts, body(): lax.all_to_all(jnp.stack([activations for _ in range(lax.axis_size('mlp')...  6.52 us
    all_to_all x1, starting transfers between devices, body(): lax.all_to_all(jnp.stack([activations for _ in range(lax.axis_size('mlp')...  4.71 us
  transfers between devices with their start and end apart: 3, of which 2 were waited for; matrix products, arithmetic and copies ran while one was open for 12% of the time, Pallas kernels for 0%

profile of v1, /device:TPU:0, one launch (start us, length us, event | category | flops | bytes accessed | tf_op | source)
XLA Modules:
  0.0 172.9 jit_solution(12294881369838541176)
XLA Ops:
  7.2 3.6 %stack.8 = bf16[8,512,512]{2,1,0:T(8,128)(2,1)} broadcast(bf16[512,512]{1,0:T(8,128)(2,1)} %param.10), dimensions={1,2} | broadcast | bytes 4718592 | tf_op jit(solution)/shard_map/stack | solution.py:96
  10.8 4.7 %all-to-all-start = ((bf16[8,512,512]{2,1,0:T(8,128)(2,1)}), bf16[8,512,512]{2,1,0:T(8,128)(2,1)}, u32[]{:S(2)}, u32[]{:S(2)}) async-start(bf16[8,512,512]{2,1,0:T(8,128)(2,1)} %stack.8), calls=%async_computation | async-start | bytes 8388608 | tf_op jit(solution)/shard_map/all_to_all | solution.py:96
  15.6 8.8 %copy.38 = bf16[4096,768]{0,1:T(8,128)(2,1)} copy(bf16[4096,768]{1,0:T(8,128)(2,1)} %param.16) | data formatting | bytes 12582912 | tf_op args[6]
  24.4 0.6 convert_reduce_fusion.1
  25.2 0.4 copy.40
  25.9 39.3 %all-to-all-done = bf16[8,512,512]{2,1,0:T(8,128)(2,1)} async-done(((bf16[8,512,512]{2,1,0:T(8,128)(2,1)}), bf16[8,512,512]{2,1,0:T(8,128)(2,1)}, u32[]{:S(2)}, u32[]{:S(2)}) %all-to-all-start) | async-done | bytes 4194336 | tf_op jit(solution)/shard_map/all_to_all | solution.py:96
  65.2 6.5 %copy.37 = bf16[8,512,512]{1,2,0:T(8,128)(2,1)} copy(bf16[8,512,512]{2,1,0:T(8,128)(2,1)} %all-to-all-done) | data formatting | bytes 8388608 | tf_op jit(solution)/shard_map/all_to_all | solution.py:96
  71.7 3.0 %convert_reduce_fusion = f32[512]{0:T(512)S(1)} fusion(bf16[8,512,512]{1,2,0:T(8,128)(2,1)} %copy.37), kind=kLoop, calls=%fused_computation.11 | loop fusion | flops 4193792 | bytes 4196352 | tf_op jit(solution)/shard_map/reduce_sum | solution.py:13
  74.6 0.5 copy-done.1
  75.1 1.2 multiply_reduce_fusion
  76.3 1.8 %add_convert_fusion = bf16[8,512,512]{1,2,0:T(8,128)(2,1)S(1)} fusion(bf16[8,512,512]{1,2,0:T(8,128)(2,1)S(1)} %copy-done.1, f32[8,512]{1,0:T(8,128)S(1)} %add.72, f32[8,512]{1,0:T(8,128)S(1)} %mul.121, f32[512]{0:T(512)S(1)} %add_rsqrt_fusion, f32[512]{0:T(512)S(1)} %broadcast_multiply_fusion), kind=kLoop, calls=%fused_computation.8 | loop fusion | flops 12582912 | bytes 8425472 | tf_op jit(solution)/shard_map/convert_element_type | solution.py:16
  78.2 3.4 %fusion.110 = f32[512,2,3,128]{0,3,2,1:T(8,128)S(1)} fusion(bf16[512,4096,1,1]{0,1,3,2:T(8,128)(2,1)S(1)} %bitcast.58, bf16[2,3,128,4096]{3,2,1,0:T(8,128)(2,1)S(1)} %bitcast.57), kind=kOutput, calls=%fused_computation.159 | convolution fusion | flops 3221225472 | bytes 12058624 | tf_op jit(solution)/shard_map/dot_general | solution.py:36
  81.9 1.0 copy-done.4
  82.9 2.4 %fusion.104 = (f32[2,512]{1,0:T(2,128)S(1)}, f32[2,512,512]{1,2,0:T(8,128)}) fusion(pred[512,512]{0,1:T(8,128)(4,1)S(1)} %copy.40, bf16[512,2,96]{0,2,1:T(8,128)(2,1)S(1)} %slice.99, bf16[512,2,32]{0,2,1:T(8,128)(2,1)S(1)} %fusion.64, bf16[512,2,96]{0,2,1:T(8,128)(2,1)S(1)} %slice.78, bf16[512,2,32]{0,2,1:T(8,128)(2,1)S(1)} %fusion.62), kind=kOutput, calls=%fused_computation.156 | convolution fusion | flops 137363968 | bytes 2887680 | tf_op jit(solution)/shard_map/sub | solution.py:54
  85.2 2.2 %convolution_convert_fusion = bf16[2,128,512]{2,1,0:T(8,128)(2,1)S(1)} fusion(f32[2,512,512]{1,2,0:T(8,128)} %get-tuple-element.16, f32[2,512]{1,0:T(2,128)S(1)} %get-tuple-element.15, f32[512,2,3,128]{0,3,2,1:T(8,128)} %copy-done.4), kind=kOutput, calls=%fused_computation.35 | convolution fusion | flops 135397376 | bytes 2625536 | tf_op jit(solution)/shard_map/hqk,khd->qhd/dot_general | solution.py:56
  87.5 0.7 copy-done.2
  88.2 2.9 %fusion.4 = bf16[512,4096]{0,1:T(8,128)(2,1)} fusion(bf16[8,512,512]{1,2,0:T(8,128)(2,1)S(1)} %copy-done.2, f32[4096]{0:T(1024)S(1)} %copy-done.6, f32[4096]{0:T(1024)S(1)} %copy-done.7, f32[512]{0:T(512)S(1)} %add_rsqrt_fusion, f32[512]{0:T(512)S(1)} %broadcast_multiply_fusion), kind=kLoop, calls=%fused_computation.7 | loop fusion | flops 12582912 | bytes 8425472 | tf_op jit(solution)/shard_map/convert_element_type | solution.py:16
  91.1 23.4 %fusion.16 = f32[512,4096]{1,0:T(8,128)} fusion(bf16[1024,4096]{1,0:T(8,128)(2,1)} %param.19, bf16[512,4096]{0,1:T(8,128)(2,1)} %fusion.4, bf16[4096,1024]{1,0:T(8,128)(2,1)} %param.18), kind=kOutput, calls=%fused_computation.36 | convolution fusion | flops 8624013312 | bytes 29360128 | tf_op jit(solution)/shard_map/dot_general | solution.py:111
  114.5 6.6 %add_convert_fusion.1 = bf16[512,4096]{1,0:T(8,128)(2,1)} fusion(f32[512,4096]{1,0:T(8,128)} %fusion.16, bf16[512,256]{0,1:T(8,128)(2,1)S(1)} %bitcast.59, bf16[256,4096]{1,0:T(8,128)(2,1)S(1)} %copy-done), kind=kOutput, calls=%fused_computation.9 | convolution fusion | flops 1077936128 | bytes 14942208 | tf_op jit(solution)/shard_map/dot_general | solution.py:111
  121.2 0.6 copy-done.10
  121.8 0.6 dynamic-slice
  122.4 1.4 dynamic-update-slice
  123.8 17.8 %all-reduce = s32[16]{0:T(128)S(1)} all-reduce(s32[16]{0:T(128)S(1)} %dynamic-update-slice), channel_id=1, replica_groups=mesh['req'=16,'mlp'=8] {'req'}, use_global_device_ids=true, to_apply=%add | all-reduce | flops 16 | bytes 128
  142.0 0.3 reduce-window.9
  142.7 2.4 %scatter_custom_fusion = s32[256]{0:T(256)S(1)} fusion(s32[512]{0:T(512)S(1)} %bitcast.61, s32[512]{0:T(512)S(1)} %iota.32, s32[]{:T(128)} %constant.46.clone.1), kind=kCustom, calls=%fused_computation.119 | custom fusion | bytes 1028 | tf_op jit(solution)/shard_map/scatter | solution.py:93
  145.2 1.1 slice.98
  147.1 1.1 copy.47
  148.2 3.6 %all-to-all-start.1 = ((bf16[32,16,512]{2,0,1:T(8,128)(2,1)}), bf16[32,16,512]{2,0,1:T(8,128)(2,1)S(1)}, u32[]{:S(2)}, u32[]{:S(2)}) async-start(bf16[32,16,512]{2,0,1:T(8,128)(2,1)} %copy.47), calls=%async_computation.2 | async-start | bytes 1048576 | tf_op jit(solution)/shard_map/all_to_all | solution.py:102
  151.8 10.1 %all-to-all-done.1 = bf16[32,16,512]{2,0,1:T(8,128)(2,1)S(1)} async-done(((bf16[32,16,512]{2,0,1:T(8,128)(2,1)}), bf16[32,16,512]{2,0,1:T(8,128)(2,1)S(1)}, u32[]{:S(2)}, u32[]{:S(2)}) %all-to-all-start.1) | async-done | bytes 524320 | tf_op jit(solution)/shard_map/all_to_all | solution.py:102
  161.8 1.2 gather_fusion
  163.1 0.7 pad_maximum_fusion.1
  163.9 2.2 %add_select_fusion = f32[512,512]{1,0:T(8,128)} fusion(bf16[512,512]{1,0:T(8,128)(2,1)} %reduce-scatter.2.cloned.1.call-done, bf16[512,512]{1,0:T(8,128)(2,1)S(1)} %copy-done.3, pred[512]{0:T(512)(128)(4,1)S(1)} %get-tuple-element.3), kind=kLoop, calls=%fused_computation.37 | loop fusion | flops 1048576 | bytes 2097664 | tf_op jit(solution)/shard_map/jit(_where)/select_n | solution.py:118
  (67 shorter events, 2.7 us)
Async XLA Ops:
  7.2 107.3 %copy-start = (bf16[256,4096]{1,0:T(8,128)(2,1)S(1)}, bf16[256,4096]{1,0:T(8,128)(2,1)}, u32[]{:S(2)}) copy-start(bf16[256,4096]{1,0:T(8,128)(2,1)} %param.17) | copy-start | bytes 6291460
  10.8 4.8 %copy-start.8 = (f32[4096]{0:T(1024)S(1)}, f32[4096]{0:T(1024)}, u32[]{:S(2)}) copy-start(f32[4096]{0:T(1024)} %param.13) | copy-start | bytes 49156
  10.8 4.8 %copy-start.9 = (f32[4096]{0:T(1024)S(1)}, f32[4096]{0:T(1024)}, u32[]{:S(2)}) copy-start(f32[4096]{0:T(1024)} %param.12) | copy-start | bytes 49156
  10.8 54.4 %all-to-all-start = ((bf16[8,512,512]{2,1,0:T(8,128)(2,1)}), bf16[8,512,512]{2,1,0:T(8,128)(2,1)}, u32[]{:S(2)}, u32[]{:S(2)}) async-start(bf16[8,512,512]{2,1,0:T(8,128)(2,1)} %stack.8), calls=%async_computation | async-start | bytes 8388608 | tf_op jit(solution)/shard_map/all_to_all | solution.py:96
  15.5 148.4 %reduce-scatter.2.cloned.1.call-start = ((), (), s32[]{:S(2)}) async-start(), calls=%async_computation.3 | async-start | bytes 4718592 | tf_op jit(solution)/shard_map/reduce_scatter | solution.py:114
  15.6 8.8 %copy-start.5 = (s32[512]{0:T(512)S(1)}, s32[512]{0:T(512)}, u32[]{:S(2)}) copy-start(s32[512]{0:T(512)} %param.11) | copy-start | bytes 6148
  71.7 3.4 %copy-start.1 = (bf16[8,512,512]{1,2,0:T(8,128)(2,1)S(1)}, bf16[8,512,512]{1,2,0:T(8,128)(2,1)}, u32[]{:S(2)}) copy-start(bf16[8,512,512]{1,2,0:T(8,128)(2,1)} %copy.37) | copy-start | bytes 12582916
  75.1 2.9 %slice-start = ((s8[6291456]{0:T(1024)(128)(4,1)}), s8[4194304]{0:T(1024)(128)(4,1)S(1)}, s32[]{:S(2)}) async-start(s8[6291456]{0:T(1024)(128)(4,1)} %bitcast.55), calls=%async_computation.4 | async-start | bytes 8388608
  76.3 1.9 %slice-start.1 = ((s8[6291456]{0:T(1024)(128)(4,1)}), s8[2097152]{0:T(1024)(128)(4,1)S(1)}, s32[]{:S(2)}) async-start(s8[6291456]{0:T(1024)(128)(4,1)} %bitcast.55), calls=%async_computation.5 | async-start | bytes 4194304
  81.6 1.2 copy-start.4
  85.2 3.0 %copy-start.2 = (bf16[8,512,512]{1,2,0:T(8,128)(2,1)S(1)}, bf16[8,512,512]{1,2,0:T(8,128)(2,1)}, u32[]{:S(2)}) copy-start(bf16[8,512,512]{1,2,0:T(8,128)(2,1)} %copy.37) | copy-start | bytes 12582916
  85.2 3.0 %copy-start.6 = (f32[4096]{0:T(1024)S(1)}, f32[4096]{0:T(1024)}, u32[]{:S(2)}) copy-start(f32[4096]{0:T(1024)} %param.15) | copy-start | bytes 49156
  85.2 3.0 %copy-start.7 = (f32[4096]{0:T(1024)S(1)}, f32[4096]{0:T(1024)}, u32[]{:S(2)}) copy-start(f32[4096]{0:T(1024)} %param.14) | copy-start | bytes 49156
  121.2 0.7 copy-start.10
  148.2 13.7 %all-to-all-start.1 = ((bf16[32,16,512]{2,0,1:T(8,128)(2,1)}), bf16[32,16,512]{2,0,1:T(8,128)(2,1)S(1)}, u32[]{:S(2)}, u32[]{:S(2)}) async-start(bf16[32,16,512]{2,0,1:T(8,128)(2,1)} %copy.47), calls=%async_computation.2 | async-start | bytes 1048576 | tf_op jit(solution)/shard_map/all_to_all | solution.py:102
  151.7 12.1 %copy-start.3 = (bf16[512,512]{1,0:T(8,128)(2,1)S(1)}, bf16[512,512]{1,0:T(8,128)(2,1)}, u32[]{:S(2)}) copy-start(bf16[512,512]{1,0:T(8,128)(2,1)} %param.10) | copy-start | bytes 1572868
Sparse Core Ops, SparseCore 0:
  121.3 38.4 reduce-scatter.1
